TPU v7x, 256 devices: a whole 4x4x8 slice. The times are simulated.
256 devices in a mesh: row: 8 (over z), col: 16 (over y, x), pan: 2 (over core).
Axes of the slice: x: 4, y: 4, z: 8, core: 2. Of those that a mesh axis runs over, the one named last changes fastest.
Arguments:
- plan_values: bfloat16 [8192, 128, 256], P('row', 'col', 'pan'), may hold values from 0.099609375 to 1
- plan_blocks: int32 [8, 128], P('row', 'col'), may hold values from 0 to 127, as said below
- first_values: bfloat16 [32, 3, 256, 256], P('row'), may hold values from -0.21875 to 0.21875
- first_blocks: int32 [32, 3], P('row'), may hold values from 0 to 3, as said below
- second_values: bfloat16 [128, 6, 256, 256], P('col', None, None, 'pan'), may hold values from -0.15625 to 0.15625
- second_blocks: int32 [128, 6], P('col'), may hold values from 0 to 7, as said below
- weight_first: float32 [8192], P('row'), may hold values from 0.5 to 2
- weight_second: float32 [128, 256], P('col', 'pan'), may hold values from 0.5 to 2
- offset_first: float32 [8192], P('row'), may hold values from -3 to 3
- offset_second: float32 [128, 256], P('col', 'pan'), may hold values from -3 to 3
Outputs:
- new_plan: bfloat16 [8192, 128, 256], P('row', 'col', 'pan')
- scale_first: float32 [8192], P('row')
- scale_second: float32 [128, 256], P('col', 'pan')
Inputs may be any that keep to these rules, and one draw needn't show every extreme that they name: `plan_blocks`: each entry is a slice-B block number; its column panel is the entry // 8. Within the 8 slots of one index of col (aligned groups of the second dimension) no column panel is named more than 2 times, and in every row panel one column panel is named exactly 2 times by every such group. `first_blocks`: block numbers within the row panel of the slice-A block; the 3 entries of a row are distinct. `second_blocks`: block numbers within the column panel of the slice-B block; the 6 entries of a row are distinct.
All inputs are finite; a program needn't handle non-finite values.
Results may differ from a plain program's by a relative error of at most 0.0087.
Values may be sent and summed in bfloat16 or wider, within the bound.
No kernel may reach another device: no remote copies, remote signals or barrier semaphores. Data moves between devices by JAX's collectives and lax.ppermute only.
A program may use at most 128 MiB of HBM per device.

v0:
```python
import jax
import jax.numpy as jnp
from jax import lax
from jax.sharding import PartitionSpec as P

CAP = 2


def first_product(plan_values, first_values, first_blocks):
    tile_count = first_blocks.shape[0]
    block_size = first_values.shape[2]
    slot_count = plan_values.shape[1]
    half_width = plan_values.shape[2]
    row_tiles = plan_values.reshape(tile_count, block_size, slot_count * half_width)
    running = jnp.zeros(row_tiles.shape, jnp.float32)
    for neighbor in range(first_blocks.shape[1]):
        picked = jnp.take(row_tiles, first_blocks[:, neighbor], axis=0)
        running = running + jnp.einsum(
            "iab,ibn->ian", first_values[:, neighbor], picked, preferred_element_type=jnp.float32
        )
    return running.astype(jnp.bfloat16).reshape(tile_count * block_size, slot_count, half_width)


def dispatch(chooser, within_panel, product):
    outgoing = jnp.einsum(
        "dcs,rsh->dcrh", chooser.astype(jnp.bfloat16), product, preferred_element_type=jnp.float32
    ).astype(jnp.bfloat16)
    labels = jnp.sum(chooser.astype(jnp.int32) * (within_panel + 1)[None, None, :], axis=2) - 1
    return (outgoing, labels)


def second_product(dense_plan, second_values, second_blocks):
    blocks_here = second_blocks.shape[0]
    columns = jnp.arange(blocks_here)
    placer = (second_blocks[:, :, None] == columns[None, None, :]).astype(jnp.bfloat16)
    panel_matrix = jnp.einsum(
        "kqbh,kql->kblh", second_values, placer, preferred_element_type=jnp.float32
    ).astype(jnp.bfloat16)
    return jnp.einsum("rkb,kblh->rlh", dense_plan, panel_matrix, preferred_element_type=jnp.float32)


def local(
    plan_values,
    plan_blocks,
    first_values,
    first_blocks,
    second_values,
    second_blocks,
    weight_first,
    weight_second,
    offset_first,
    offset_second,
):
    col_count = lax.axis_size("col")
    blocks_here = second_blocks.shape[0]
    slot_count = plan_values.shape[1]
    block_size = first_values.shape[2]
    panel_rows = plan_values.shape[0]
    plan_width = float(slot_count * col_count * block_size)
    named_blocks = plan_blocks[0]
    target_panel = named_blocks // blocks_here
    within_panel = named_blocks % blocks_here
    same_panel = target_panel[:, None] == target_panel[None, :]
    earlier = jnp.arange(slot_count)[:, None] > jnp.arange(slot_count)[None, :]
    position = jnp.sum((same_panel & earlier).astype(jnp.int32), axis=1)
    chooser = (target_panel[None, None, :] == jnp.arange(col_count)[:, None, None]) & (
        position[None, None, :] == jnp.arange(CAP)[None, :, None]
    )
    product = first_product(plan_values, first_values, first_blocks)
    outgoing, labels = dispatch(chooser, within_panel, product)
    incoming, arrival_ids = (
        lax.all_to_all(outgoing, "col", split_axis=0, concat_axis=0, tiled=True),
        lax.all_to_all(labels, "col", split_axis=0, concat_axis=0, tiled=True),
    )
    item_rows = incoming.shape[2]
    arrivals = incoming.reshape(col_count * CAP, item_rows, incoming.shape[3])
    matcher = (arrival_ids.reshape(-1)[:, None] == jnp.arange(blocks_here)[None, :]).astype(
        jnp.bfloat16
    )
    dense_plan = jnp.einsum(
        "ik,irh->rkh", matcher, arrivals, preferred_element_type=jnp.float32
    ).astype(jnp.bfloat16)
    present = jnp.minimum(jnp.sum(matcher.astype(jnp.float32), axis=0), 1.0)
    gathered = lax.all_gather(dense_plan, "pan", axis=2, tiled=True)
    crossed = second_product(gathered, second_values, second_blocks)
    kernel_values = present[None, :, None] * jnp.exp(
        crossed - offset_first[:, None, None] - offset_second[None]
    )
    row_totals = lax.psum(jnp.sum(kernel_values, axis=(1, 2)), ("col", "pan"))
    scale_first = weight_first * plan_width / row_totals
    weighted = kernel_values * scale_first[:, None, None]
    colsum, counts = lax.psum((jnp.sum(weighted, axis=0), present * float(panel_rows)), "row")
    scale_second = weight_second * counts[:, None] / jnp.where(counts[:, None] > 0, colsum, 1.0)
    new_values = (weighted * scale_second[None]).astype(jnp.bfloat16)
    returned = jnp.einsum(
        "ik,rkh->irh", matcher, new_values, preferred_element_type=jnp.float32
    ).astype(jnp.bfloat16)
    returned = returned.reshape(col_count, CAP, item_rows, returned.shape[2])
    homeward = lax.all_to_all(returned, "col", split_axis=0, concat_axis=0, tiled=True)
    new_plan = jnp.einsum(
        "dcs,dcrh->rsh", chooser.astype(jnp.bfloat16), homeward, preferred_element_type=jnp.float32
    ).astype(jnp.bfloat16)
    return (new_plan, scale_first, scale_second)


def solution(mesh):
    return jax.shard_map(
        local,
        mesh=mesh,
        in_specs=(
            P("row", "col", "pan"),
            P("row", "col"),
            P("row", None, None, None),
            P("row", None),
            P("col", None, None, "pan"),
            P("col", None),
            P("row"),
            P("col", "pan"),
            P("row"),
            P("col", "pan"),
        ),
        out_specs=(P("row", "col", "pan"), P("row"), P("col", "pan")),
        check_vma=False,
    )
```

profile of v0, /device:TPU:2, one launch (start us, length us, event | category | flops | bytes accessed | tf_op | source)
XLA Modules:
  0.0 442.7 jit_solution(4532502949180978923)
XLA Ops:
  7.2 0.8 fusion.59
  8.0 0.8 fusion.60
  9.2 0.7 copy.46
  9.8 7.5 %all-to-all-start = ((s32[16,1,2]{2,1,0:T(1,128)}), s32[16,1,2]{2,1,0:T(1,128)S(1)}, u32[]{:S(2)}, u32[]{:S(2)}) async-start(s32[16,1,2]{2,1,0:T(1,128)} %copy.46), calls=%async_computation | async-start | bytes 16384 | tf_op jit(solution)/shard_map/all_to_all | solution.py:73
  17.3 1.0 slice_reduce_fusion.1
  18.4 4.2 reshape.172
  22.6 3.6 gather_fusion.1
  26.1 3.6 gather_fusion.2
  29.7 3.6 gather_fusion
  33.3 2.8 fusion.20
  36.2 1.0 fusion.22
  37.3 0.5 copy-done.2
  37.8 2.7 fusion.29
  40.5 4.0 copy.53
  44.5 2.2 copy.72
  46.7 5.1 %convolution_convert_fusion.1 = bf16[16,2,1024,128]{3,0,2,1:T(8,128)(2,1)} fusion(bf16[1024,8,128,1]{2,1,0,3:T(8,128)(2,1)S(1)} %bitcast.93, pred[2,8]{1,0:T(4,128)(4,1)S(1)} %iota_compare_fusion.4, pred[16,8]{0,1:T(8,128)(4,1)S(1)} %iota_compare_fusion.3), kind=kOutput, calls=%fused_computation.8 | convolution fusion | flops 71303424 | bytes 10485904 | tf_op jit(solution)/shard_map/dcs,rsh->dcrh/dot_general | solution.py:25
  51.8 8.8 %copy.54 = bf16[16,2,1024,128]{3,2,1,0:T(8,128)(2,1)} copy(bf16[16,2,1024,128]{3,0,2,1:T(8,128)(2,1)} %convolution_convert_fusion.1) | data formatting | bytes 16777216 | tf_op jit(solution)/shard_map/convert_element_type | solution.py:27
  60.6 7.2 %all-to-all-start.1 = ((bf16[16,2,1024,128]{3,2,1,0:T(8,128)(2,1)}), bf16[16,2,1024,128]{3,2,1,0:T(8,128)(2,1)}, u32[]{:S(2)}, u32[]{:S(2)}) async-start(bf16[16,2,1024,128]{3,2,1,0:T(8,128)(2,1)} %copy.54), calls=%async_computation.1 | async-start | bytes 16777216 | tf_op jit(solution)/shard_map/all_to_all | solution.py:72
  68.6 0.7 reduce.9
  69.3 118.5 %all-to-all-done.1 = bf16[16,2,1024,128]{3,2,1,0:T(8,128)(2,1)} async-done(((bf16[16,2,1024,128]{3,2,1,0:T(8,128)(2,1)}), bf16[16,2,1024,128]{3,2,1,0:T(8,128)(2,1)}, u32[]{:S(2)}, u32[]{:S(2)}) %all-to-all-start.1) | async-done | bytes 8388640 | tf_op jit(solution)/shard_map/all_to_all | solution.py:72
  187.9 9.3 %convert_bitcast_fusion.1 = bf16[1024,8,128]{2,1,0:T(8,128)(2,1)} fusion(bf16[32,1024,128]{2,1,0:T(8,128)(2,1)} %bitcast.10, s32[32]{0:T(128)S(1)} %eq.91), kind=kOutput, calls=%fused_computation.31 | convolution fusion | flops 68157696 | bytes 10485888 | tf_op jit(solution)/shard_map/ik,irh->rkh/dot_general | solution.py:80
  197.3 4.0 convert_bitcast_fusion
  201.3 18.2 %all-gather.2.cloned.1.call-done = bf16[1024,8,256]{2,1,0:T(8,128)(2,1)} async-done(((bf16[1024,8,128]{2,1,0:T(8,128)(2,1)}), bf16[1024,8,256]{2,1,0:T(8,128)(2,1)}) %all-gather.2.cloned.1.call-update) | async-done | bytes 4194320 | tf_op jit(solution)/shard_map/all_gather | solution.py:84
  219.5 10.1 %fusion.15 = (f32[1024]{0:T(1024)S(1)}, f32[1024,8,128,1]{2,0,3,1:T(8,128)}) fusion(f32[8,128]{1,0:T(8,128)S(1)} %copy-done.7, f32[1024]{0:T(1024)S(1)} %copy-done.8, f32[8]{0:T(128)S(1)} %get-tuple-element.10, bf16[8,256,8,128]{3,2,1,0:T(8,128)(2,1)} %convert_bitcast_fusion, bf16[1024,8,256]{2,1,0:T(8,128)(2,1)} %all-gather.2.cloned.1.call-done), kind=kOutput, calls=%fused_computation.24 | convolution fusion | flops 4299160576 | bytes 12595232 | tf_op jit(solution)/shard_map/rkb,kblh->rlh/dot_general | solution.py:39
  229.6 62.6 %psum.21 = f32[1024]{0:T(1024)S(1)} all-reduce(f32[1024]{0:T(1024)S(1)} %get-tuple-element.13), channel_id=1, replica_groups=mesh['row'=8,'col'=16,'pan'=2] {'col','pan'}, use_global_device_ids=true, to_apply=%region_4.6 | all-reduce | flops 1024 | bytes 8192 | tf_op jit(solution)/shard_map/psum | solution.py:89
  292.2 3.3 multiply_reduce_fusion
  295.5 17.7 %all-reduce = (f32[8,128]{1,0:T(8,128)S(1)}, f32[8]{0:T(128)S(1)}) all-reduce(f32[8,128]{1,0:T(8,128)S(1)} %multiply_reduce_fusion, f32[8]{0:T(128)S(1)} %get-tuple-element.9), channel_id=1, replica_groups=mesh['row'=8,'col'=16,'pan'=2] {'row'}, use_global_device_ids=true, to_apply=%region_7.9 | all-reduce | flops 1032 | bytes 8256 | tf_op jit(solution)/shard_map/psum | solution.py:92
  313.3 3.8 multiply_convert_fusion
  317.2 6.3 %convolution_convert_fusion = bf16[32,1024,128]{2,0,1:T(8,128)(2,1)S(1)} fusion(bf16[1024,8,128]{2,0,1:T(8,128)(2,1)S(1)} %multiply_convert_fusion, s32[32]{0:T(128)S(1)} %eq.91), kind=kOutput, calls=%fused_computation.7 | convolution fusion | flops 71303424 | bytes 10485888 | tf_op jit(solution)/shard_map/ik,rkh->irh/dot_general | solution.py:95
  323.5 8.0 %copy.60 = bf16[16,2,1024,128]{3,1,2,0:T(2,128)(2,1)S(1)} copy(bf16[16,2,1024,128]{3,1,0,2:T(2,128)(2,1)S(1)} %bitcast.91) | data formatting | bytes 16777216 | tf_op jit(solution)/shard_map/reshape | solution.py:98
  331.5 98.3 %all_to_all.16 = bf16[16,2,1024,128]{3,1,2,0:T(2,128)(2,1)S(1)} all-to-all(bf16[16,2,1024,128]{3,1,2,0:T(2,128)(2,1)S(1)} %copy.60), channel_id=1, replica_groups=mesh['row'=8,'col'=16,'pan'=2] {'col'}, dimensions={0} | all-to-all | bytes 16777216 | tf_op jit(solution)/shard_map/all_to_all | solution.py:99
  429.9 6.0 %fusion.32 = bf16[1024,8,128]{2,1,0:T(8,128)(2,1)} fusion(bf16[16,2,1024,128]{3,1,2,0:T(2,128)(2,1)S(1)} %all_to_all.16, pred[2,8]{1,0:T(4,128)(4,1)S(1)} %iota_compare_fusion.4, pred[16,8]{0,1:T(8,128)(4,1)S(1)} %iota_compare_fusion.3), kind=kOutput, calls=%fused_computation.36 | convolution fusion | flops 68157696 | bytes 10485904 | tf_op jit(solution)/shard_map/dcs,dcrh->rsh/dot_general | solution.py:100
  (45 shorter events, 1.5 us)
Async XLA Ops:
  7.2 190.1 %copy-start = (bf16[8,6,256,128]{3,2,1,0:T(8,128)(2,1)S(1)}, bf16[8,6,256,128]{3,2,1,0:T(8,128)(2,1)}, u32[]{:S(2)}) copy-start(bf16[8,6,256,128]{3,2,1,0:T(8,128)(2,1)} %param.16) | copy-start | bytes 9437188
  9.8 50.8 %all-to-all-start = ((s32[16,1,2]{2,1,0:T(1,128)}), s32[16,1,2]{2,1,0:T(1,128)S(1)}, u32[]{:S(2)}, u32[]{:S(2)}) async-start(s32[16,1,2]{2,1,0:T(1,128)} %copy.46), calls=%async_computation | async-start | bytes 16384 | tf_op jit(solution)/shard_map/all_to_all | solution.py:73
  33.3 2.8 copy-start.3
  33.3 2.8 copy-start.4
  36.2 1.6 copy-start.2
  60.6 127.3 %all-to-all-start.1 = ((bf16[16,2,1024,128]{3,2,1,0:T(8,128)(2,1)}), bf16[16,2,1024,128]{3,2,1,0:T(8,128)(2,1)}, u32[]{:S(2)}, u32[]{:S(2)}) async-start(bf16[16,2,1024,128]{3,2,1,0:T(8,128)(2,1)} %copy.54), calls=%async_computation.1 | async-start | bytes 16777216 | tf_op jit(solution)/shard_map/all_to_all | solution.py:72
  67.8 151.7 %all-gather.2.cloned.1.call-start = ((), (), s32[]{:S(2)}) async-start(), calls=%async_computation.3 | async-start | bytes 6291456 | tf_op jit(solution)/shard_map/all_gather | solution.py:84
  187.9 9.4 %copy-start.9 = (s32[8,6]{1,0:T(8,128)S(1)}, s32[8,6]{1,0:T(8,128)}, u32[]{:S(2)}) copy-start(s32[8,6]{1,0:T(8,128)} %param.17) | copy-start | bytes 580
  197.2 22.3 %copy-start.7 = (f32[8,128]{1,0:T(8,128)S(1)}, f32[8,128]{1,0:T(8,128)}, u32[]{:S(2)}) copy-start(f32[8,128]{1,0:T(8,128)} %param.21) | copy-start | bytes 12292
  197.3 22.3 %copy-start.8 = (f32[1024]{0:T(1024)S(1)}, f32[1024]{0:T(1024)}, u32[]{:S(2)}) copy-start(f32[1024]{0:T(1024)} %param.20) | copy-start | bytes 12292
  219.5 72.7 %copy-start.10 = (f32[1024]{0:T(1024)S(1)}, f32[1024]{0:T(1024)}, u32[]{:S(2)}) copy-start(f32[1024]{0:T(1024)} %param.18) | copy-start | bytes 12292
  229.6 83.6 %copy-start.11 = (f32[8,128]{1,0:T(8,128)S(1)}, f32[8,128]{1,0:T(8,128)}, u32[]{:S(2)}) copy-start(f32[8,128]{1,0:T(8,128)} %param.19) | copy-start | bytes 12292
  292.2 24.9 %copy-start.5 = (f32[1024]{0:T(1024)}, f32[1024]{0:T(1024)S(1)}, u32[]{:S(2)}) copy-start(f32[1024]{0:T(1024)S(1)} %multiply_divide_fusion) | copy-start | bytes 12292
  313.3 10.2 %copy-start.6 = (f32[8,128]{1,0:T(8,128)}, f32[8,128]{1,0:T(8,128)S(1)}, u32[]{:S(2)}) copy-start(f32[8,128]{1,0:T(8,128)S(1)} %select_divide_fusion) | copy-start | bytes 12292
  331.5 104.3 %copy-start.1 = (bf16[8,6,256,128]{3,2,1,0:T(8,128)(2,1)S(1)}, bf16[8,6,256,128]{3,2,1,0:T(8,128)(2,1)}, u32[]{:S(2)}) copy-start(bf16[8,6,256,128]{3,2,1,0:T(8,128)(2,1)} %param.16) | copy-start | bytes 9437188
Sparse Core Ops, SparseCore 0:
  197.3 22.1 all-gather.1
where the time goes:
time: 443 us
  blocking collectives  179 us (40%)
  waiting for transfers between devices  137 us (31%)
  matrix products  47.4 us (11%)
  local copies, waits for them, and re-layouts  40.8 us (9%)
  starting transfers between devices  14.9 us (3%)
  between operations  14.3 us (3%)
  other arithmetic  10 us (2%)
    all_to_all x1, waiting for transfers between devices, local(): lax.all_to_all(outgoing, 'col', split_axis=0, concat_axis=0, tiled=True)  119 us
    all_to_all x1, blocking collectives, local(): lax.all_to_all(returned, 'col', split_axis=0, concat_axis=0, tiled=True)  98.3 us
    psum x1, blocking collectives, local(): row_totals = lax.psum(jnp.sum(kernel_values, axis=(1, 2)), ('col', 'pan'))  62.6 us
    all_gather x1, waiting for transfers between devices, local(): gathered = lax.all_gather(dense_plan, 'pan', axis=2, tiled=True)  18.2 us
    psum x1, blocking collectives, local(): lax.psum((jnp.sum(weighted, axis=0), present * float(panel_rows)), 'row')  17.7 us
    gather x3, local copies, waits for them, and re-layouts, first_product(): picked = jnp.take(row_tiles, first_blocks[:, neighbor], axis=0)  10.8 us
    dot_general x1, matrix products, second_product(): jnp.einsum('rkb,kblh->rlh', dense_plan, panel_matrix, preferred_element_t...  10.1 us
    dot_general x1, matrix products, local(): jnp.einsum('ik,irh->rkh', matcher, arrivals, preferred_element_type=jnp.f...  9.33 us
  transfers between devices with their start and end apart: 3, of which 2 were waited for; matrix products, arithmetic and copies ran while one was open for 11% of the time, Pallas kernels for 0%

commit v1 on v0

--- a/solution.py
+++ b/solution.py
@@ -1,9 +1,18 @@
+import functools
 import jax
 import jax.numpy as jnp
 from jax import lax
 from jax.sharding import PartitionSpec as P
 
 CAP = 2
+
+
+def mark_threads_on_mesh(block_in, axis_name):
+    g_now = lax.all_gather(block_in, axis_name).sum(axis=0)
+    return g_now
+
+
+lots_all_balance = functools.partial(mark_threads_on_mesh, axis_name=("col", "pan"))
 
 
 def first_product(plan_values, first_values, first_blocks):
@@ -86,7 +95,7 @@
     kernel_values = present[None, :, None] * jnp.exp(
         crossed - offset_first[:, None, None] - offset_second[None]
     )
-    row_totals = lax.psum(jnp.sum(kernel_values, axis=(1, 2)), ("col", "pan"))
+    row_totals = lots_all_balance(jnp.sum(kernel_values, axis=(1, 2)))
     scale_first = weight_first * plan_width / row_totals
     weighted = kernel_values * scale_first[:, None, None]
     colsum, counts = lax.psum((jnp.sum(weighted, axis=0), present * float(panel_rows)), "row")

time: 443 us -> 404 us (0.912)
  blocking collectives: 179 us -> 139 us
    psum x1 -> x0, blocking collectives: 62.6 us -> none  [local(): row_totals = lax.psum(jnp.sum(kernel_values, axis=(1, 2)), ('col', 'pan'))]
    all_gather x0 -> x1, blocking collectives: none -> 24.7 us  [mark_threads_on_mesh(): g_now = lax.all_gather(block_in, axis_name).sum(axis=0)]
  transfers between devices with their start and end apart: 3 -> 3, of which waited for: 2 -> 2; matrix products, arithmetic and copies ran while one was open for 11% -> 12% of each run, Pallas kernels for 0% -> 0%
where the time goes in v1:
time: 404 us; the launch traced here: 403 us
  blocking collectives  139 us (34%)
  waiting for transfers between devices  137 us (34%)
  matrix products  47.4 us (12%)
  local copies, waits for them, and re-layouts  40.8 us (10%)
  starting transfers between devices  14.9 us (4%)
  between operations  14.3 us (4%)
  other arithmetic  10 us (2%)
    all_to_all x1, waiting for transfers between devices, local(): lax.all_to_all(outgoing, 'col', split_axis=0, concat_axis=0, tiled=True)  119 us
    all_to_all x1, blocking collectives, local(): lax.all_to_all(returned, 'col', split_axis=0, concat_axis=0, tiled=True)  96.8 us
    all_gather x1, blocking collectives, mark_threads_on_mesh(): g_now = lax.all_gather(block_in, axis_name).sum(axis=0)  24.7 us
    all_gather x1, waiting for transfers between devices, local(): gathered = lax.all_gather(dense_plan, 'pan', axis=2, tiled=True)  18.2 us
    psum x1, blocking collectives, local(): lax.psum((jnp.sum(weighted, axis=0), present * float(panel_rows)), 'row')  17.7 us
    gather x3, local copies, waits for them, and re-layouts, first_product(): picked = jnp.take(row_tiles, first_blocks[:, neighbor], axis=0)  10.8 us
    dot_general x1, matrix products, second_product(): jnp.einsum('rkb,kblh->rlh', dense_plan, panel_matrix, preferred_element_t...  10.1 us
    dot_general x1, matrix products, local(): jnp.einsum('ik,irh->rkh', matcher, arrivals, preferred_element_type=jnp.f...  9.33 us
  transfers between devices with their start and end apart: 3, of which 2 were waited for; matrix products, arithmetic and copies ran while one was open for 12% of the time, Pallas kernels for 0%

profile of v1, /device:TPU:2, one launch (start us, length us, event | category | flops | bytes accessed | tf_op | source)
XLA Modules:
  0.0 403.4 jit_solution(6317270987980212334)
XLA Ops:
  7.2 0.8 fusion.59
  8.0 0.8 fusion.60
  9.2 0.7 copy.46
  9.8 7.5 %all-to-all-start = ((s32[16,1,2]{2,1,0:T(1,128)}), s32[16,1,2]{2,1,0:T(1,128)S(1)}, u32[]{:S(2)}, u32[]{:S(2)}) async-start(s32[16,1,2]{2,1,0:T(1,128)} %copy.46), calls=%async_computation | async-start | bytes 16384 | tf_op jit(solution)/shard_map/all_to_all | solution.py:82
  17.3 1.0 slice_reduce_fusion.1
  18.4 4.2 %reshape.172 = bf16[4,256,1024]{2,1,0:T(8,128)(2,1)} reshape(bf16[1024,8,128]{2,1,0:T(8,128)(2,1)} %param.12) | data formatting | bytes 4194304 | tf_op jit(solution)/shard_map/reshape | solution.py:23
  22.6 3.6 gather_fusion.1
  26.1 3.6 gather_fusion.2
  29.7 3.6 gather_fusion
  33.3 2.8 fusion.20
  36.2 1.0 fusion.22
  37.3 0.5 copy-done.2
  37.8 2.7 fusion.29
  40.5 4.0 copy.53
  44.5 2.2 copy.72
  46.7 5.1 %convolution_convert_fusion.1 = bf16[16,2,1024,128]{3,0,2,1:T(8,128)(2,1)} fusion(bf16[1024,8,128,1]{2,1,0,3:T(8,128)(2,1)S(1)} %bitcast.93, pred[2,8]{1,0:T(4,128)(4,1)S(1)} %iota_compare_fusion.4, pred[16,8]{0,1:T(8,128)(4,1)S(1)} %iota_compare_fusion.3), kind=kOutput, calls=%fused_computation.8 | convolution fusion | flops 71303424 | bytes 10485904 | tf_op jit(solution)/shard_map/dcs,rsh->dcrh/dot_general | solution.py:34
  51.8 8.8 %copy.54 = bf16[16,2,1024,128]{3,2,1,0:T(8,128)(2,1)} copy(bf16[16,2,1024,128]{3,0,2,1:T(8,128)(2,1)} %convolution_convert_fusion.1) | data formatting | bytes 16777216 | tf_op jit(solution)/shard_map/convert_element_type | solution.py:36
  60.6 7.2 %all-to-all-start.1 = ((bf16[16,2,1024,128]{3,2,1,0:T(8,128)(2,1)}), bf16[16,2,1024,128]{3,2,1,0:T(8,128)(2,1)}, u32[]{:S(2)}, u32[]{:S(2)}) async-start(bf16[16,2,1024,128]{3,2,1,0:T(8,128)(2,1)} %copy.54), calls=%async_computation.1 | async-start | bytes 16777216 | tf_op jit(solution)/shard_map/all_to_all | solution.py:81
  68.6 0.7 reduce.9
  69.3 118.5 %all-to-all-done.1 = bf16[16,2,1024,128]{3,2,1,0:T(8,128)(2,1)} async-done(((bf16[16,2,1024,128]{3,2,1,0:T(8,128)(2,1)}), bf16[16,2,1024,128]{3,2,1,0:T(8,128)(2,1)}, u32[]{:S(2)}, u32[]{:S(2)}) %all-to-all-start.1) | async-done | bytes 8388640 | tf_op jit(solution)/shard_map/all_to_all | solution.py:81
  187.9 9.3 %convert_bitcast_fusion.1 = bf16[1024,8,128]{2,1,0:T(8,128)(2,1)} fusion(bf16[32,1024,128]{2,1,0:T(8,128)(2,1)} %bitcast.10, s32[32]{0:T(128)S(1)} %eq.91), kind=kOutput, calls=%fused_computation.31 | convolution fusion | flops 68157696 | bytes 10485888 | tf_op jit(solution)/shard_map/ik,irh->rkh/dot_general | solution.py:89
  197.3 4.0 convert_bitcast_fusion
  201.3 18.2 %all-gather.3.cloned.1.call-done = bf16[1024,8,256]{2,1,0:T(8,128)(2,1)} async-done(((bf16[1024,8,128]{2,1,0:T(8,128)(2,1)}), bf16[1024,8,256]{2,1,0:T(8,128)(2,1)}) %all-gather.3.cloned.1.call-update) | async-done | bytes 4194320 | tf_op jit(solution)/shard_map/all_gather | solution.py:93
  219.5 10.1 %fusion.15 = (f32[1024]{0:T(1024)S(1)}, f32[1024,8,128,1]{2,0,3,1:T(8,128)}) fusion(f32[8,128]{1,0:T(8,128)S(1)} %copy-done.7, f32[1024]{0:T(1024)S(1)} %copy-done.8, f32[8]{0:T(128)S(1)} %get-tuple-element.10, bf16[8,256,8,128]{3,2,1,0:T(8,128)(2,1)} %convert_bitcast_fusion, bf16[1024,8,256]{2,1,0:T(8,128)(2,1)} %all-gather.3.cloned.1.call-done), kind=kOutput, calls=%fused_computation.24 | convolution fusion | flops 4299160576 | bytes 12595232 | tf_op jit(solution)/shard_map/rkb,kblh->rlh/dot_general | solution.py:48
  229.6 24.7 %all-gather = f32[32768]{0:T(1024)S(1)} all-gather(f32[1024]{0:T(1024)S(1)} %get-tuple-element.13), channel_id=2, replica_groups=mesh['row'=8,'col'=16,'pan'=2] {'col','pan'}, dimensions={0}, use_global_device_ids=true | all-gather | bytes 135168 | tf_op jit(solution)/shard_map/all_gather | solution.py:11
  254.4 3.3 multiply_reduce_fusion
  257.7 17.7 %all-reduce = (f32[8,128]{1,0:T(8,128)S(1)}, f32[8]{0:T(128)S(1)}) all-reduce(f32[8,128]{1,0:T(8,128)S(1)} %multiply_reduce_fusion, f32[8]{0:T(128)S(1)} %get-tuple-element.9), channel_id=1, replica_groups=mesh['row'=8,'col'=16,'pan'=2] {'row'}, use_global_device_ids=true, to_apply=%region_7.9 | all-reduce | flops 1032 | bytes 8256 | tf_op jit(solution)/shard_map/psum | solution.py:101
  275.5 3.8 multiply_convert_fusion
  279.4 6.3 %convolution_convert_fusion = bf16[32,1024,128]{2,0,1:T(8,128)(2,1)S(1)} fusion(bf16[1024,8,128]{2,0,1:T(8,128)(2,1)S(1)} %multiply_convert_fusion, s32[32]{0:T(128)S(1)} %eq.91), kind=kOutput, calls=%fused_computation.7 | convolution fusion | flops 71303424 | bytes 10485888 | tf_op jit(solution)/shard_map/ik,rkh->irh/dot_general | solution.py:104
  285.7 8.0 %copy.60 = bf16[16,2,1024,128]{3,1,2,0:T(2,128)(2,1)S(1)} copy(bf16[16,2,1024,128]{3,1,0,2:T(2,128)(2,1)S(1)} %bitcast.91) | data formatting | bytes 16777216 | tf_op jit(solution)/shard_map/reshape | solution.py:107
  293.7 96.8 %all_to_all.16 = bf16[16,2,1024,128]{3,1,2,0:T(2,128)(2,1)S(1)} all-to-all(bf16[16,2,1024,128]{3,1,2,0:T(2,128)(2,1)S(1)} %copy.60), channel_id=1, replica_groups=mesh['row'=8,'col'=16,'pan'=2] {'col'}, dimensions={0} | all-to-all | bytes 16777216 | tf_op jit(solution)/shard_map/all_to_all | solution.py:108
  390.5 6.0 %fusion.32 = bf16[1024,8,128]{2,1,0:T(8,128)(2,1)} fusion(bf16[16,2,1024,128]{3,1,2,0:T(2,128)(2,1)S(1)} %all_to_all.16, pred[2,8]{1,0:T(4,128)(4,1)S(1)} %iota_compare_fusion.4, pred[16,8]{0,1:T(8,128)(4,1)S(1)} %iota_compare_fusion.3), kind=kOutput, calls=%fused_computation.36 | convolution fusion | flops 68157696 | bytes 10485904 | tf_op jit(solution)/shard_map/dcs,dcrh->rsh/dot_general | solution.py:109
  (47 shorter events, 1.6 us)
Async XLA Ops:
  7.2 190.1 %copy-start = (bf16[8,6,256,128]{3,2,1,0:T(8,128)(2,1)S(1)}, bf16[8,6,256,128]{3,2,1,0:T(8,128)(2,1)}, u32[]{:S(2)}) copy-start(bf16[8,6,256,128]{3,2,1,0:T(8,128)(2,1)} %param.16) | copy-start | bytes 9437188
  9.8 50.8 %all-to-all-start = ((s32[16,1,2]{2,1,0:T(1,128)}), s32[16,1,2]{2,1,0:T(1,128)S(1)}, u32[]{:S(2)}, u32[]{:S(2)}) async-start(s32[16,1,2]{2,1,0:T(1,128)} %copy.46), calls=%async_computation | async-start | bytes 16384 | tf_op jit(solution)/shard_map/all_to_all | solution.py:82
  33.3 2.8 copy-start.3
  33.3 2.8 copy-start.4
  36.2 1.6 copy-start.2
  60.6 127.3 %all-to-all-start.1 = ((bf16[16,2,1024,128]{3,2,1,0:T(8,128)(2,1)}), bf16[16,2,1024,128]{3,2,1,0:T(8,128)(2,1)}, u32[]{:S(2)}, u32[]{:S(2)}) async-start(bf16[16,2,1024,128]{3,2,1,0:T(8,128)(2,1)} %copy.54), calls=%async_computation.1 | async-start | bytes 16777216 | tf_op jit(solution)/shard_map/all_to_all | solution.py:81
  67.8 151.7 %all-gather.3.cloned.1.call-start = ((), (), s32[]{:S(2)}) async-start(), calls=%async_computation.3 | async-start | bytes 6291456 | tf_op jit(solution)/shard_map/all_gather | solution.py:93
  187.9 9.4 %copy-start.9 = (s32[8,6]{1,0:T(8,128)S(1)}, s32[8,6]{1,0:T(8,128)}, u32[]{:S(2)}) copy-start(s32[8,6]{1,0:T(8,128)} %param.17) | copy-start | bytes 580
  197.2 22.3 %copy-start.7 = (f32[8,128]{1,0:T(8,128)S(1)}, f32[8,128]{1,0:T(8,128)}, u32[]{:S(2)}) copy-start(f32[8,128]{1,0:T(8,128)} %param.21) | copy-start | bytes 12292
  197.3 22.3 %copy-start.8 = (f32[1024]{0:T(1024)S(1)}, f32[1024]{0:T(1024)}, u32[]{:S(2)}) copy-start(f32[1024]{0:T(1024)} %param.20) | copy-start | bytes 12292
  219.5 34.9 %copy-start.10 = (f32[1024]{0:T(1024)S(1)}, f32[1024]{0:T(1024)}, u32[]{:S(2)}) copy-start(f32[1024]{0:T(1024)} %param.18) | copy-start | bytes 12292
  229.6 45.8 %copy-start.11 = (f32[8,128]{1,0:T(8,128)S(1)}, f32[8,128]{1,0:T(8,128)}, u32[]{:S(2)}) copy-start(f32[8,128]{1,0:T(8,128)} %param.19) | copy-start | bytes 12292
  254.4 25.0 %copy-start.5 = (f32[1024]{0:T(1024)}, f32[1024]{0:T(1024)S(1)}, u32[]{:S(2)}) copy-start(f32[1024]{0:T(1024)S(1)} %multiply_divide_fusion) | copy-start | bytes 12292
  275.5 10.2 %copy-start.6 = (f32[8,128]{1,0:T(8,128)}, f32[8,128]{1,0:T(8,128)S(1)}, u32[]{:S(2)}) copy-start(f32[8,128]{1,0:T(8,128)S(1)} %select_divide_fusion) | copy-start | bytes 12292
  293.7 102.8 %copy-start.1 = (bf16[8,6,256,128]{3,2,1,0:T(8,128)(2,1)S(1)}, bf16[8,6,256,128]{3,2,1,0:T(8,128)(2,1)}, u32[]{:S(2)}) copy-start(bf16[8,6,256,128]{3,2,1,0:T(8,128)(2,1)} %param.16) | copy-start | bytes 9437188
Sparse Core Ops, SparseCore 0:
  197.3 22.1 all-gather.2
